TPU v7x, 256 devices: a whole 4x4x8 slice. The times are simulated.
256 devices in a mesh: seq: 32 (over z, x), expert: 8 (over y, core).
Axes of the slice: x: 4, y: 4, z: 8, core: 2. Of those that a mesh axis runs over, the one named last changes fastest.
Arguments:
- tokens: bfloat16 [4096, 4096], P('seq'), may hold values from -6 to 6
- norm_gain: float32 [4096], replicated, may hold values from 0.1 to 1.9
- router_weight: bfloat16 [4096, 8], replicated, may hold values from -0.09375 to 0.09375
- expert_ids: int32 [4096, 2], P('seq'), may hold values from 0 to 7, all different within a row; in each aligned block of 128 rows (0 to 127, 128 to 255, ...) at most 40 rows name the same one
- gate_weight: bfloat16 [8, 4096, 8192], P('expert', None, 'seq'), may hold values from -0.09375 to 0.09375
- up_weight: bfloat16 [8, 4096, 8192], P('expert', None, 'seq'), may hold values from -0.09375 to 0.09375
- down_weight: bfloat16 [8, 8192, 4096], P('expert', 'seq'), may hold values from -0.0625 to 0.0625
- query_weight: bfloat16 [4096, 2048], P(None, 'expert'), may hold values from -0.09375 to 0.09375
- key_weight: bfloat16 [4096, 2048], P(None, 'expert'), may hold values from -0.09375 to 0.09375
- log_decay: float32 [32, 4096], P('expert', 'seq'), may hold values from -1.5 to 0
- carried_state: float32 [32, 64, 128], P('expert'), may hold values from -48 to 48
- out_gain: float32 [4096], P('expert'), may hold values from 0.1 to 1.9
Outputs:
- teacher_out: bfloat16 [4096, 4096], P('seq', 'expert')
- student_out: bfloat16 [4096, 4096], P('seq', 'expert')
- token_loss: float32 [4096], P('seq')
Inputs may be any that keep to these rules, and one draw needn't show every extreme that they name: `expert_ids`: each token names 2 different experts. Among the 128 tokens of one block no expert is named by more than 40 tokens, and in every draw some expert is named by exactly 40 tokens of some block.
All inputs are finite; a program needn't handle non-finite values.
Results may differ from a plain program's by a relative error of at most 0.01.
Values may be sent and summed in bfloat16 or wider, within the bound.
No kernel may reach another device: no remote copies, remote signals or barrier semaphores. Data moves between devices by JAX's collectives and lax.ppermute only.
A program may use at most 128 MiB of HBM per device.

v0:
```python
import jax
import jax.numpy as jnp
from jax import lax
from jax.sharding import Mesh
from jax.sharding import PartitionSpec as P

SEQ = ("seq_0", "seq_1")
norm_epsilon = 1e-05
head_epsilon = 1e-06
peak_error = lax.Precision.HIGHEST


def sum_by_axis(terms, axes):
    running = terms.astype(jnp.bfloat16)
    for axis in axes:
        running = lax.psum_scatter(running, axis, scatter_dimension=0, tiled=True)
    return running.astype(jnp.float32)


def filled_with(value, identity):
    return jax.tree.map(
        lambda a, e: jnp.broadcast_to(jnp.asarray(e, a.dtype), a.shape), value, identity
    )


def prefix_by_axis(value, axes, combine, identity):
    before = start = filled_with(value, identity)
    running = value
    for axis in reversed(axes):
        peers, here = (lax.axis_size(axis), lax.axis_index(axis))
        pieces = jax.tree.map(
            lambda part, kind: lax.all_gather(part.astype(kind), axis),
            running,
            (jnp.bfloat16, jnp.bfloat16),
        )
        inside, running = (start, start)
        for k in range(peers):
            passed = k < here
            running = combine(
                running, jax.tree.map(lambda part, own: part[k].astype(own.dtype), pieces, value)
            )
            inside = jax.tree.map(lambda new, old: jnp.where(passed, new, old), running, inside)
        before = combine(inside, before)
    return before


def copy_for_each(value, axis):
    copies = jnp.broadcast_to(value, (lax.axis_size(axis), *value.shape))
    return lax.all_to_all(copies, axis, split_axis=0, concat_axis=0, tiled=True)


def over_copies(value, axis):
    return copy_for_each(value, axis).sum(axis=0)


def on_device(
    tokens,
    norm_gain,
    router_weight,
    expert_ids,
    gate_weight,
    up_weight,
    down_weight,
    query_weight,
    key_weight,
    log_decay,
    carried_state,
    out_gain,
):
    span_rows = tokens.shape[0]
    width = tokens.shape[1]
    expert_count = router_weight.shape[1]
    top_count = expert_ids.shape[1]
    capacity = 7 * top_count * span_rows // (8 * expert_count)
    groups = lax.axis_size("expert")
    mine = lax.axis_index("expert")
    block_cols = width // groups
    tok_float = tokens.astype(jnp.float32)
    normed = (
        tok_float
        * lax.rsqrt(jnp.mean(tok_float * tok_float, axis=1, keepdims=True) + norm_epsilon)
        * norm_gain
    ).astype(jnp.bfloat16)
    logits = jnp.dot(normed, router_weight, preferred_element_type=jnp.float32)
    expert_iota = jnp.arange(expert_count, dtype=jnp.int32)
    picks = expert_ids[:, :, None] == expert_iota[None, None, :]
    chosen = jnp.sum(jnp.where(picks, logits[:, None, :], jnp.float32(0.0)), axis=2)
    first_share = 1.0 / (1.0 + jnp.exp(chosen[:, 1] - chosen[:, 0]))
    shares = jnp.stack([first_share, 1.0 - first_share], axis=1)
    mix_weight = jnp.sum(jnp.where(picks, shares[:, :, None], jnp.float32(0.0)), axis=1)
    hits = jnp.any(picks, axis=1).astype(jnp.int32)
    slots = jnp.cumsum(hits, axis=0) - hits
    slot_iota = jnp.arange(capacity, dtype=jnp.int32)
    own_col = expert_iota[None, :] == mine
    own_hits = jnp.sum(jnp.where(own_col, hits, 0), axis=1)
    own_slots = jnp.sum(jnp.where(own_col, slots, 0), axis=1)
    select_own = (own_hits[None, :] == 1) & (own_slots[None, :] == slot_iota[:, None])
    dispatched = jnp.dot(
        select_own.astype(jnp.bfloat16), normed, preferred_element_type=jnp.float32
    ).astype(jnp.bfloat16)
    piece_rows = lax.all_gather(dispatched, SEQ, axis=0, tiled=True)
    gate_proj = jnp.dot(piece_rows, gate_weight[0], preferred_element_type=jnp.float32)
    up_proj = jnp.dot(piece_rows, up_weight[0], preferred_element_type=jnp.float32)
    hidden = (jax.nn.silu(gate_proj) * up_proj).astype(jnp.bfloat16)
    partial_value = jnp.dot(hidden, down_weight[0], preferred_element_type=jnp.float32).astype(
        jnp.bfloat16
    )
    partial_value = lax.optimization_barrier(partial_value)
    summed = sum_by_axis(partial_value.astype(jnp.float32), SEQ)
    expert_half = lax.optimization_barrier(summed.astype(jnp.bfloat16))
    pieces = expert_half.reshape(1, capacity, groups, block_cols)
    arrived = lax.all_to_all(pieces, "expert", split_axis=2, concat_axis=0, tiled=True).reshape(
        groups, capacity, block_cols
    )
    select_all = (hits.T[:, None, :] == 1) & (slots.T[:, None, :] == slot_iota[None, :, None])
    weigh_all = select_all.astype(jnp.float32) * mix_weight.T[:, None, :]
    mixed = jnp.einsum("ept,epd->td", weigh_all, arrived.astype(jnp.float32), precision=peak_error)
    tok_cols = lax.dynamic_slice_in_dim(tok_float, mine * block_cols, block_cols, 1)
    teacher_hidden = tok_cols + mixed
    heads_local = log_decay.shape[0]
    key_size = query_weight.shape[1] // heads_local
    head_size = block_cols // heads_local
    query_rows = (
        jnp.dot(tokens, query_weight, preferred_element_type=jnp.float32)
        .reshape(span_rows, heads_local, key_size)
        .transpose(1, 0, 2)
    )
    keys_proj = (
        jnp.dot(tokens, key_weight, preferred_element_type=jnp.float32)
        .reshape(span_rows, heads_local, key_size)
        .transpose(1, 0, 2)
    )
    value_rows = tok_cols.reshape(span_rows, heads_local, head_size).transpose(1, 0, 2)
    running_state = jnp.cumsum(log_decay, axis=1)
    last_state = running_state[:, -1]
    lower = jnp.arange(span_rows)[:, None] >= jnp.arange(span_rows)[None, :]
    gaps = running_state[:, :, None] - running_state[:, None, :]
    weights = jnp.where(lower[None], jnp.exp(jnp.minimum(gaps, 0.0)), 0.0)
    scores = jnp.einsum("htk,hsk->hts", query_rows, keys_proj, precision=peak_error) * weights
    output_rows = jnp.einsum("hts,hsv->htv", scores, value_rows, precision=peak_error)
    scaled_keys = keys_proj * jnp.exp(last_state[:, None] - running_state)[:, :, None]
    block_state = jnp.einsum("wpl,wpg->wlg", scaled_keys, value_rows, precision=peak_error)
    retain = jnp.exp(last_state)

    def join(earlier, later):
        return (earlier[0] * later[0], later[0][:, None, None] * earlier[1] + later[1])

    kept_before, prior_state = prefix_by_axis(
        (retain, block_state), SEQ, join, (jnp.ones_like(retain), jnp.zeros_like(block_state))
    )
    prior_state = prior_state + kept_before[:, None, None] * carried_state
    output_rows = output_rows + jnp.exp(running_state)[:, :, None] * jnp.einsum(
        "ezy,eyl->ezl", query_rows, prior_state, precision=peak_error
    )
    normed_out = output_rows * lax.rsqrt(
        jnp.mean(output_rows * output_rows, axis=2, keepdims=True) + head_epsilon
    )
    branch = normed_out.transpose(1, 0, 2).reshape(span_rows, block_cols) * out_gain
    student_hidden = tok_cols + branch
    gap = student_hidden - teacher_hidden
    token_loss = over_copies(jnp.sum(gap * gap, axis=1), "expert") / width
    return (teacher_hidden.astype(jnp.bfloat16), student_hidden.astype(jnp.bfloat16), token_loss)


def solution(mesh):
    finer = Mesh(mesh.devices.reshape(8, 4, mesh.shape["expert"]), ("seq_0", "seq_1", "expert"))
    in_specs = (
        P(SEQ, None),
        P(),
        P(),
        P(SEQ, None),
        P("expert", None, SEQ),
        P("expert", None, SEQ),
        P("expert", SEQ, None),
        P(None, "expert"),
        P(None, "expert"),
        P("expert", SEQ),
        P("expert", None, None),
        P("expert"),
    )
    out_specs = (P(SEQ, "expert"), P(SEQ, "expert"), P(SEQ))
    return jax.shard_map(
        on_device, mesh=finer, in_specs=in_specs, out_specs=out_specs, check_vma=False
    )
```

profile of v0, /device:TPU:1, one launch (start us, length us, event | category | flops | bytes accessed | tf_op | source)
XLA Modules:
  0.0 289.6 jit_solution(5486637954161039477)
XLA Ops:
  7.2 0.8 fusion.111
  8.5 1.5 multiply_reduce_fusion
  10.0 2.4 fusion.1
  12.5 101.8 %all-gather.6.cloned.1.call-done = bf16[32,28,4096]{2,1,0:T(8,128)(2,1)} async-done(((bf16[1,28,4096]{2,1,0:T(8,128)(2,1)}), bf16[32,28,4096]{2,1,0:T(8,128)(2,1)}) %all-gather.6.cloned.1.call-update) | async-done | bytes 7340048 | tf_op jit(solution)/shard_map/all_gather | solution.py:101
  114.3 9.0 %reshape.357 = bf16[896,4096]{1,0:T(8,128)(2,1)} reshape(bf16[32,28,4096]{2,1,0:T(8,128)(2,1)} %all-gather.6.cloned.1.call-done) | data formatting | bytes 14680064
  123.4 5.7 %fusion.5 = f32[896,256]{1,0:T(8,128)S(1)} fusion(bf16[896,4096]{1,0:T(8,128)(2,1)} %reshape.357, bf16[1,4096,256]{2,1,0:T(8,128)(2,1)} %param.16), kind=kOutput, calls=%fused_computation.6 | convolution fusion | flops 1879048192 | bytes 10354688 | tf_op jit(solution)/shard_map/dot_general | solution.py:102
  129.1 15.1 %convolution_convert_fusion = bf16[896,4096]{1,0:T(8,128)(2,1)} fusion(bf16[1,256,4096]{2,1,0:T(8,128)(2,1)S(1)} %copy-done, bf16[896,4096]{1,0:T(8,128)(2,1)} %reshape.357, bf16[1,4096,256]{2,1,0:T(8,128)(2,1)} %param.17, f32[896,256]{1,0:T(8,128)S(1)} %fusion.5), kind=kOutput, calls=%fused_computation | convolution fusion | flops 3763142656 | bytes 19791872 | tf_op jit(solution)/shard_map/dot_general | solution.py:105
  146.9 6.8 %all-reduce = bf16[16]{0:T(256)(128)(2,1)S(1)} all-reduce(bf16[16]{0:T(256)(128)(2,1)S(1)} %dynamic-update-slice), channel_id=2, replica_groups=mesh['seq_0'=8,'seq_1'=4,'expert'=8] {'seq_1'}, use_global_device_ids=true, to_apply=%add | all-reduce | flops 16 | bytes 64
  153.8 12.4 %all-gather.3 = bf16[8,1,4]{2,1,0:T(2,128)(2,1)S(1)} all-gather(bf16[1,1,4]{2,1,0:T(2,128)(2,1)S(1)} %fusion.124), channel_id=1, replica_groups=mesh['seq_0'=8,'seq_1'=4,'expert'=8] {'seq_0'}, dimensions={0}, use_global_device_ids=true | all-gather | bytes 72 | tf_op jit(solution)/shard_map/all_gather | solution.py:32
  166.6 2.5 fusion.132
  169.5 10.8 %all-gather.1 = bf16[16,64,128]{2,1,0:T(8,128)(2,1)S(1)} all-gather(bf16[4,64,128]{2,1,0:T(8,128)(2,1)S(1)} %convolution_convert_fusion.2), channel_id=3, replica_groups=mesh['seq_0'=8,'seq_1'=4,'expert'=8] {'seq_1'}, dimensions={0}, use_global_device_ids=true | all-gather | bytes 327680 | tf_op jit(solution)/shard_map/all_gather | solution.py:32
  181.2 24.9 %all_gather.26 = bf16[8,4,64,128]{3,2,1,0:T(8,128)(2,1)S(1)} all-gather(bf16[1,4,64,128]{3,2,1,0:T(8,128)(2,1)S(1)} %fusion.42), channel_id=1, replica_groups=mesh['seq_0'=8,'seq_1'=4,'expert'=8] {'seq_0'}, dimensions={0}, use_global_device_ids=true | all-gather | bytes 589824 | tf_op jit(solution)/shard_map/all_gather | solution.py:32
  206.1 1.0 fusion.131
  207.7 0.9 fusion.33
  209.8 22.2 %reduce-scatter.4.cloned.1.call-done = bf16[112,4096]{1,0:T(8,128)(2,1)} async-done(((bf16[896,4096]{1,0:T(8,128)(2,1)}), bf16[112,4096]{1,0:T(8,128)(2,1)}) %reduce-scatter.4.cloned.1.call-update) | async-done | bytes 917520 | tf_op jit(solution)/shard_map/reduce_scatter | solution.py:16
  231.9 18.4 %fusion = bf16[32,4096]{1,0:T(8,128)(2,1)S(1)} fusion(bf16[112,4096]{1,0:T(8,128)(2,1)} %reduce-scatter.4.cloned.1.call-done), kind=kCustom, calls=%all-reduce-scatter | all-reduce-scatter fusion | flops 524289 | bytes 1180672
  251.1 2.0 collective-permute-start
  253.1 1.6 convert_element_type.322
  254.7 1.1 copy.68
  256.6 1.4 concatenate
  259.0 6.8 %all-to-all-start = ((bf16[1,28,8,512]{3,1,0,2:T(8,128)(2,1)}), bf16[1,28,8,512]{3,1,0,2:T(8,128)(2,1)S(1)}, u32[]{:S(2)}, u32[]{:S(2)}) async-start(bf16[1,28,8,512]{3,1,0,2:T(8,128)(2,1)} %copy.58), calls=%async_computation.1 | async-start | bytes 524288 | tf_op jit(solution)/shard_map/all_to_all | solution.py:112
  265.8 6.5 %all-to-all-done = bf16[1,28,8,512]{3,1,0,2:T(8,128)(2,1)S(1)} async-done(((bf16[1,28,8,512]{3,1,0,2:T(8,128)(2,1)}), bf16[1,28,8,512]{3,1,0,2:T(8,128)(2,1)S(1)}, u32[]{:S(2)}, u32[]{:S(2)}) %all-to-all-start) | async-done | bytes 229408 | tf_op jit(solution)/shard_map/all_to_all | solution.py:112
  272.3 1.9 multiply_reduce_fusion.1
  274.2 8.0 %all_to_all.21 = f32[8,1,128]{2,1,0:T(1,128)S(1)} all-to-all(f32[8,1,128]{2,1,0:T(1,128)S(1)} %broadcast_in_dim.62), channel_id=1, replica_groups=mesh['seq_0'=8,'seq_1'=4,'expert'=8] {'expert'}, dimensions={0} | all-to-all | bytes 8192 | tf_op jit(solution)/shard_map/all_to_all | solution.py:49
  (69 shorter events, 8.4 us)
Async XLA Ops:
  7.2 121.9 %copy-start = (bf16[1,256,4096]{2,1,0:T(8,128)(2,1)S(1)}, bf16[1,256,4096]{2,1,0:T(8,128)(2,1)}, u32[]{:S(2)}) copy-start(bf16[1,256,4096]{2,1,0:T(8,128)(2,1)} %param.18) | copy-start | bytes 6291460
  7.2 107.2 %all-gather.6.cloned.1.call-start = ((), (), s32[]{:S(2)}) async-start(), calls=%async_computation.4 | async-start | bytes 8650752 | tf_op jit(solution)/shard_map/all_gather | solution.py:101
  12.5 219.4 %reduce-scatter.4.cloned.1.call-start = ((), (), s32[]{:S(2)}) async-start(), calls=%async_computation.3 | async-start | bytes 8257536 | tf_op jit(solution)/shard_map/reduce_scatter | solution.py:16
  144.2 0.7 copy-start.6
  144.2 1.9 copy-start.5
  144.2 22.0 %copy-start.1 = (bf16[128,4096]{1,0:T(8,128)(2,1)S(1)}, bf16[128,4096]{1,0:T(8,128)(2,1)}, u32[]{:S(2)}) copy-start(bf16[128,4096]{1,0:T(8,128)(2,1)} %param.12) | copy-start | bytes 3145732
  166.2 14.2 %copy-start.9 = (f32[4096]{0:T(1024)S(1)}, f32[4096]{0:T(1024)}, u32[]{:S(2)}) copy-start(f32[4096]{0:T(1024)} %param.13) | copy-start | bytes 49156
  166.3 14.0 %copy-start.8 = (bf16[4096,8]{0,1:T(8,128)(2,1)S(1)}, bf16[4096,8]{0,1:T(8,128)(2,1)}, u32[]{:S(2)}) copy-start(bf16[4096,8]{0,1:T(8,128)(2,1)} %param.14) | copy-start | bytes 196612
  169.1 11.7 %copy-start.3 = (s32[128,2]{0,1:T(2,128)S(1)}, s32[128,2]{0,1:T(2,128)}, u32[]{:S(2)}) copy-start(s32[128,2]{0,1:T(2,128)} %param.15) | copy-start | bytes 3076
  169.1 36.9 %copy-start.2 = (bf16[4096,256]{1,0:T(8,128)(2,1)S(1)}, bf16[4096,256]{1,0:T(8,128)(2,1)}, u32[]{:S(2)}) copy-start(bf16[4096,256]{1,0:T(8,128)(2,1)} %param.19) | copy-start | bytes 6291460
  181.2 26.5 %copy-start.7 = (f32[4,64,128]{2,1,0:T(8,128)S(1)}, f32[4,64,128]{2,1,0:T(8,128)}, u32[]{:S(2)}) copy-start(f32[4,64,128]{2,1,0:T(8,128)} %param.22) | copy-start | bytes 393220
  251.1 5.5 %collective-permute-start = (bf16[12,4096]{1,0:T(8,128)(2,1)}, bf16[12,4096]{1,0:T(8,128)(2,1)}, u32[]{:S(2)}, u32[]{:S(2)}) collective-permute-start(bf16[12,4096]{1,0:T(8,128)(2,1)} %slice.151), channel_id=1, source_target_pairs={{0,8},{8,16},{16,24},{1,9},{9,17},{17,25},{2,10},{10,18},{18,26},{... | collective-permute-start | bytes 294920
  254.7 17.6 %copy-start.4 = (f32[512]{0:T(512)S(1)}, f32[512]{0:T(512)}, u32[]{:S(2)}) copy-start(f32[512]{0:T(512)} %param.23) | copy-start | bytes 6148
  259.0 13.3 %all-to-all-start = ((bf16[1,28,8,512]{3,1,0,2:T(8,128)(2,1)}), bf16[1,28,8,512]{3,1,0,2:T(8,128)(2,1)S(1)}, u32[]{:S(2)}, u32[]{:S(2)}) async-start(bf16[1,28,8,512]{3,1,0,2:T(8,128)(2,1)} %copy.58), calls=%async_computation.1 | async-start | bytes 524288 | tf_op jit(solution)/shard_map/all_to_all | solution.py:112
Sparse Core Ops, SparseCore 0:
  12.6 101.6 all-gather.5
  144.3 87.5 reduce-scatter.3
where the time goes:
time: 290 us
  waiting for transfers between devices  130 us (45%)
  blocking collectives  81.3 us (28%)
  matrix products  31.4 us (11%)
  between operations  15.7 us (5%)
  local copies, waits for them, and re-layouts  15.3 us (5%)
  starting transfers between devices  8.9 us (3%)
  other arithmetic  6.56 us (2%)
    all_gather x1, waiting for transfers between devices, on_device(): piece_rows = lax.all_gather(dispatched, SEQ, axis=0, tiled=True)  102 us
    all_gather x3, blocking collectives, prefix_by_axis(): lax.all_gather(part.astype(kind), axis)  48.1 us
    unnamed x2, blocking collectives  25.3 us
    reduce_scatter x1, waiting for transfers between devices, sum_by_axis(): running = lax.psum_scatter(running, axis, scatter_dimension=0, tiled=True)  22.2 us
    dot_general x1, matrix products, on_device(): jnp.dot(hidden, down_weight[0], preferred_element_type=jnp.float32)  15.1 us
    unnamed x28, local copies, waits for them, and re-layouts  12.8 us
    all_to_all x1, blocking collectives, copy_for_each(): return lax.all_to_all(copies, axis, split_axis=0, concat_axis=0, tiled=True)  7.96 us
    all_to_all x1, starting transfers between devices, on_device(): lax.all_to_all(pieces, 'expert', split_axis=2, concat_axis=0, tiled=True)  6.81 us
  transfers between devices with their start and end apart: 4, of which 3 were waited for; matrix products, arithmetic and copies ran while one was open for 4% of the time, Pallas kernels for 0%

commit v1 on v0

--- a/solution.py
+++ b/solution.py
@@ -98,7 +98,9 @@
     dispatched = jnp.dot(
         select_own.astype(jnp.bfloat16), normed, preferred_element_type=jnp.float32
     ).astype(jnp.bfloat16)
-    piece_rows = lax.all_gather(dispatched, SEQ, axis=0, tiled=True)
+    piece_rows = jnp.concatenate(
+        lax.all_to_all(jnp.stack([dispatched] * lax.axis_size(SEQ)), SEQ, 0, 0), axis=0
+    )
     gate_proj = jnp.dot(piece_rows, gate_weight[0], preferred_element_type=jnp.float32)
     up_proj = jnp.dot(piece_rows, up_weight[0], preferred_element_type=jnp.float32)
     hidden = (jax.nn.silu(gate_proj) * up_proj).astype(jnp.bfloat16)

time: 290 us -> 386 us (1.33)
  blocking collectives: 81.3 us -> 279 us
  waiting for transfers between devices: 130 us -> 28.2 us
    all_to_all x0 -> x1, blocking collectives: none -> 195 us  [on_device(): lax.all_to_all(jnp.stack([dispatched] * lax.axis_size(SEQ)), SEQ, 0, 0)]
    all_gather x1 -> x0, waiting for transfers between devices: 102 us -> none  [on_device(): piece_rows = lax.all_gather(dispatched, SEQ, axis=0, tiled=True)]
    reshape x0 -> x1, local copies, waits for them, and re-layouts: none -> 9.03 us  [on_device(): jnp.concatenate(lax.all_to_all(jnp.stack([dispatched] * lax.axis_size(SEQ...]
    unnamed x28 -> x27, local copies, waits for them, and re-layouts: 12.8 us -> 3.77 us
  transfers between devices with their start and end apart: 4 -> 3, of which waited for: 3 -> 2; matrix products, arithmetic and copies ran while one was open for 4% -> 3% of each run, Pallas kernels for 0% -> 0%
where the time goes in v1:
time: 386 us; the launch traced here: 385 us
  blocking collectives  279 us (72%)
  matrix products  30.7 us (8%)
  waiting for transfers between devices  28.2 us (7%)
  local copies, waits for them, and re-layouts  16.3 us (4%)
  between operations  15.7 us (4%)
  starting transfers between devices  8.82 us (2%)
  other arithmetic  6.56 us (2%)
    all_to_all x1, blocking collectives, on_device(): lax.all_to_all(jnp.stack([dispatched] * lax.axis_size(SEQ)), SEQ, 0, 0)  195 us
    all_gather x3, blocking collectives, prefix_by_axis(): lax.all_gather(part.astype(kind), axis)  48 us
    unnamed x2, blocking collectives  27.7 us
    reduce_scatter x1, waiting for transfers between devices, sum_by_axis(): running = lax.psum_scatter(running, axis, scatter_dimension=0, tiled=True)  21.7 us
    dot_general x1, matrix products, on_device(): jnp.dot(hidden, down_weight[0], preferred_element_type=jnp.float32)  15.1 us
    reshape x1, local copies, waits for them, and re-layouts, on_device(): jnp.concatenate(lax.all_to_all(jnp.stack([dispatched] * lax.axis_size(SEQ...  9.03 us
    all_to_all x1, blocking collectives, copy_for_each(): return lax.all_to_all(copies, axis, split_axis=0, concat_axis=0, tiled=True)  7.95 us
  transfers between devices with their start and end apart: 3, of which 2 were waited for; matrix products, arithmetic and copies ran while one was open for 3% of the time, Pallas kernels for 0%

profile of v1, /device:TPU:1, one launch (start us, length us, event | category | flops | bytes accessed | tf_op | source)
XLA Modules:
  0.0 385.2 jit_solution(1271900288786791718)
XLA Ops:
  8.5 1.5 multiply_reduce_fusion
  10.0 1.7 convolution_convert_fusion.1
  11.8 1.0 stack.5
  12.8 195.3 %all_to_all.26 = bf16[32,28,4096]{2,1,0:T(8,128)(2,1)} all-to-all(bf16[32,28,4096]{2,1,0:T(8,128)(2,1)S(1)} %stack.5), channel_id=1, replica_groups=mesh['seq_0'=8,'seq_1'=4,'expert'=8] {'seq_0','seq_1'}, dimensions={0} | all-to-all | bytes 14680064 | tf_op jit(solution)/shard_map/all_to_all | solution.py:102
  208.1 9.0 %reshape.300 = bf16[896,4096]{1,0:T(8,128)(2,1)} reshape(bf16[32,28,4096]{2,1,0:T(8,128)(2,1)} %all_to_all.26) | data formatting | bytes 14680064 | tf_op jit(solution)/shard_map/reshape | solution.py:101
  217.1 5.7 %fusion.4 = f32[896,256]{1,0:T(8,128)S(1)} fusion(bf16[896,4096]{1,0:T(8,128)(2,1)} %reshape.300, bf16[1,4096,256]{2,1,0:T(8,128)(2,1)} %param.16), kind=kOutput, calls=%fused_computation.5 | convolution fusion | flops 1879048192 | bytes 10354688 | tf_op jit(solution)/shard_map/dot_general | solution.py:104
  222.9 15.1 %convolution_convert_fusion = bf16[896,4096]{1,0:T(8,128)(2,1)} fusion(bf16[1,256,4096]{2,1,0:T(8,128)(2,1)S(1)} %copy-done, bf16[896,4096]{1,0:T(8,128)(2,1)} %reshape.300, bf16[1,4096,256]{2,1,0:T(8,128)(2,1)} %param.17, f32[896,256]{1,0:T(8,128)S(1)} %fusion.4), kind=kOutput, calls=%fused_computation | convolution fusion | flops 3763142656 | bytes 19791872 | tf_op jit(solution)/shard_map/dot_general | solution.py:107
  240.6 9.2 %all-reduce = bf16[16]{0:T(256)(128)(2,1)S(1)} all-reduce(bf16[16]{0:T(256)(128)(2,1)S(1)} %dynamic-update-slice), channel_id=2, replica_groups=mesh['seq_0'=8,'seq_1'=4,'expert'=8] {'seq_1'}, use_global_device_ids=true, to_apply=%add | all-reduce | flops 16 | bytes 64
  249.9 12.2 %all-gather.2 = bf16[8,1,4]{2,1,0:T(2,128)(2,1)S(1)} all-gather(bf16[1,1,4]{2,1,0:T(2,128)(2,1)S(1)} %fusion.123), channel_id=1, replica_groups=mesh['seq_0'=8,'seq_1'=4,'expert'=8] {'seq_0'}, dimensions={0}, use_global_device_ids=true | all-gather | bytes 72 | tf_op jit(solution)/shard_map/all_gather | solution.py:32
  262.6 2.6 fusion.131
  265.5 10.7 %all-gather.1 = bf16[16,64,128]{2,1,0:T(8,128)(2,1)S(1)} all-gather(bf16[4,64,128]{2,1,0:T(8,128)(2,1)S(1)} %convolution_convert_fusion.2), channel_id=3, replica_groups=mesh['seq_0'=8,'seq_1'=4,'expert'=8] {'seq_1'}, dimensions={0}, use_global_device_ids=true | all-gather | bytes 327680 | tf_op jit(solution)/shard_map/all_gather | solution.py:32
  277.1 25.0 %all_gather.22 = bf16[8,4,64,128]{3,2,1,0:T(8,128)(2,1)S(1)} all-gather(bf16[1,4,64,128]{3,2,1,0:T(8,128)(2,1)S(1)} %fusion.41), channel_id=1, replica_groups=mesh['seq_0'=8,'seq_1'=4,'expert'=8] {'seq_0'}, dimensions={0}, use_global_device_ids=true | all-gather | bytes 589824 | tf_op jit(solution)/shard_map/all_gather | solution.py:32
  302.1 1.0 fusion.130
  303.7 0.9 fusion.32
  305.8 21.7 %reduce-scatter.4.cloned.1.call-done = bf16[112,4096]{1,0:T(8,128)(2,1)} async-done(((bf16[896,4096]{1,0:T(8,128)(2,1)}), bf16[112,4096]{1,0:T(8,128)(2,1)}) %reduce-scatter.4.cloned.1.call-update) | async-done | bytes 917520 | tf_op jit(solution)/shard_map/reduce_scatter | solution.py:16
  327.5 18.5 %fusion = bf16[32,4096]{1,0:T(8,128)(2,1)S(1)} fusion(bf16[112,4096]{1,0:T(8,128)(2,1)} %reduce-scatter.4.cloned.1.call-done), kind=kCustom, calls=%all-reduce-scatter | all-reduce-scatter fusion | flops 524289 | bytes 1180672
  346.7 2.0 collective-permute-start
  348.7 1.6 convert_element_type.322
  350.2 1.1 copy.68
  352.2 1.4 concatenate
  354.6 6.8 %all-to-all-start.1 = ((bf16[1,28,8,512]{3,1,0,2:T(8,128)(2,1)}), bf16[1,28,8,512]{3,1,0,2:T(8,128)(2,1)S(1)}, u32[]{:S(2)}, u32[]{:S(2)}) async-start(bf16[1,28,8,512]{3,1,0,2:T(8,128)(2,1)} %copy.58), calls=%async_computation.2 | async-start | bytes 524288 | tf_op jit(solution)/shard_map/all_to_all | solution.py:114
  361.4 6.5 %all-to-all-done.1 = bf16[1,28,8,512]{3,1,0,2:T(8,128)(2,1)S(1)} async-done(((bf16[1,28,8,512]{3,1,0,2:T(8,128)(2,1)}), bf16[1,28,8,512]{3,1,0,2:T(8,128)(2,1)S(1)}, u32[]{:S(2)}, u32[]{:S(2)}) %all-to-all-start.1) | async-done | bytes 229408 | tf_op jit(solution)/shard_map/all_to_all | solution.py:114
  367.9 2.0 multiply_reduce_fusion.1
  369.9 8.0 %all_to_all.27 = f32[8,1,128]{2,1,0:T(1,128)S(1)} all-to-all(f32[8,1,128]{2,1,0:T(1,128)S(1)} %broadcast_in_dim.62), channel_id=1, replica_groups=mesh['seq_0'=8,'seq_1'=4,'expert'=8] {'expert'}, dimensions={0} | all-to-all | bytes 8192 | tf_op jit(solution)/shard_map/all_to_all | solution.py:49
  (68 shorter events, 9.1 us)
Async XLA Ops:
  7.2 215.7 %copy-start = (bf16[1,256,4096]{2,1,0:T(8,128)(2,1)S(1)}, bf16[1,256,4096]{2,1,0:T(8,128)(2,1)}, u32[]{:S(2)}) copy-start(bf16[1,256,4096]{2,1,0:T(8,128)(2,1)} %param.18) | copy-start | bytes 6291460
  7.2 320.3 %reduce-scatter.4.cloned.1.call-start = ((), (), s32[]{:S(2)}) async-start(), calls=%async_computation.4 | async-start | bytes 8257536 | tf_op jit(solution)/shard_map/reduce_scatter | solution.py:16
  237.9 0.7 copy-start.6
  237.9 1.9 copy-start.5
  237.9 24.2 %copy-start.1 = (bf16[128,4096]{1,0:T(8,128)(2,1)S(1)}, bf16[128,4096]{1,0:T(8,128)(2,1)}, u32[]{:S(2)}) copy-start(bf16[128,4096]{1,0:T(8,128)(2,1)} %param.12) | copy-start | bytes 3145732
  262.2 14.1 %copy-start.9 = (f32[4096]{0:T(1024)S(1)}, f32[4096]{0:T(1024)}, u32[]{:S(2)}) copy-start(f32[4096]{0:T(1024)} %param.13) | copy-start | bytes 49156
  262.3 13.9 %copy-start.8 = (bf16[4096,8]{0,1:T(8,128)(2,1)S(1)}, bf16[4096,8]{0,1:T(8,128)(2,1)}, u32[]{:S(2)}) copy-start(bf16[4096,8]{0,1:T(8,128)(2,1)} %param.14) | copy-start | bytes 196612
  265.1 11.5 %copy-start.3 = (s32[128,2]{0,1:T(2,128)S(1)}, s32[128,2]{0,1:T(2,128)}, u32[]{:S(2)}) copy-start(s32[128,2]{0,1:T(2,128)} %param.15) | copy-start | bytes 3076
  265.1 36.9 %copy-start.2 = (bf16[4096,256]{1,0:T(8,128)(2,1)S(1)}, bf16[4096,256]{1,0:T(8,128)(2,1)}, u32[]{:S(2)}) copy-start(bf16[4096,256]{1,0:T(8,128)(2,1)} %param.19) | copy-start | bytes 6291460
  277.0 26.7 %copy-start.7 = (f32[4,64,128]{2,1,0:T(8,128)S(1)}, f32[4,64,128]{2,1,0:T(8,128)}, u32[]{:S(2)}) copy-start(f32[4,64,128]{2,1,0:T(8,128)} %param.22) | copy-start | bytes 393220
  346.7 5.4 %collective-permute-start = (bf16[12,4096]{1,0:T(8,128)(2,1)}, bf16[12,4096]{1,0:T(8,128)(2,1)}, u32[]{:S(2)}, u32[]{:S(2)}) collective-permute-start(bf16[12,4096]{1,0:T(8,128)(2,1)} %slice.151), channel_id=1, source_target_pairs={{0,8},{8,16},{16,24},{1,9},{9,17},{17,25},{2,10},{10,18},{18,26},{... | collective-permute-start | bytes 294920
  350.2 17.7 %copy-start.4 = (f32[512]{0:T(512)S(1)}, f32[512]{0:T(512)}, u32[]{:S(2)}) copy-start(f32[512]{0:T(512)} %param.23) | copy-start | bytes 6148
  354.6 13.3 %all-to-all-start.1 = ((bf16[1,28,8,512]{3,1,0,2:T(8,128)(2,1)}), bf16[1,28,8,512]{3,1,0,2:T(8,128)(2,1)S(1)}, u32[]{:S(2)}, u32[]{:S(2)}) async-start(bf16[1,28,8,512]{3,1,0,2:T(8,128)(2,1)} %copy.58), calls=%async_computation.2 | async-start | bytes 524288 | tf_op jit(solution)/shard_map/all_to_all | solution.py:114
Sparse Core Ops, SparseCore 0:
  238.1 89.3 reduce-scatter.3
